TPU v7x, 32 devices: a whole 2x2x4 slice. The times are simulated.
32 devices in a mesh: groups: 2 (over y), bx: 4 (over z), by: 2 (over x), bz: 2 (over core).
Axes of the slice: x: 2, y: 2, z: 4, core: 2. Of those that a mesh axis runs over, the one named last changes fastest.
Arguments:
- slab: float32 [4, 512, 1024], P(('groups', 'bz'), 'bx', 'by'), parts along dimension 0, may hold values from -6 to 6
- plane_test: float32 [2, 256], P('bz'), may hold values from -4 to 4
- row_test: float32 [512, 256], P('bx'), may hold values from -0.25 to 0.25
- col_test: float32 [1024, 256], P('by'), may hold values from -0.1875 to 0.1875
- core_planes: float32 [512, 2], P('bz'), may hold values from -4 to 4
- core_rows: float32 [512, 512], P(None, 'bx'), may hold values from -0.25 to 0.25
- core_cols: float32 [512, 1024], P(None, 'by'), may hold values from -0.1875 to 0.1875
Outputs:
- plane_sketch: float32 [4, 256], P(('groups', 'bz')), parts along dimension 0
- row_sketch: float32 [1024, 256], P(('groups', 'bx'), ('by', 'bz')), parts along dimension 0
- col_sketch: float32 [2048, 256], P(('groups', 'by'), ('bx', 'bz')), parts along dimension 0
- core_sketch: float32 [1024, 512, 512], P(('groups', 'bz'), 'bx', 'by'), parts along dimension 0
There are 2 independent parts, one for each index of `groups`. A program takes and returns all parts, laid end to end along the dimension named above; an argument that names none is the same for every part. Nothing has to cross between parts.
All inputs are finite; a program needn't handle non-finite values.
Results may differ from a plain program's by a relative error of at most 0.00011.
Values sent between devices are 32-bit elements; how exact they have to be, the bound alone decides.
A program may use at most 128 MiB of HBM per device.

v0:
```python
import jax
import jax.numpy as jnp
from jax import lax
from jax.sharding import PartitionSpec as P


def on_device(slab, plane_test, row_test, col_test, core_planes, core_rows, core_cols):
    highest = lax.Precision.HIGHEST
    by_col = jnp.einsum("pij,jr->pir", slab, col_test, precision=highest)
    plane_part = jnp.einsum("pir,ir->pr", by_col, row_test, precision=highest)
    row_part = jnp.einsum("pir,pr->ir", by_col, plane_test, precision=highest)
    by_row = jnp.einsum("pij,ir->pjr", slab, row_test, precision=highest)
    col_part = jnp.einsum("pjr,pr->jr", by_row, plane_test, precision=highest)
    plane_sketch = lax.psum(plane_part, ("bx", "by"))
    row_sketch = lax.psum_scatter(row_part, ("by", "bz"), scatter_dimension=1, tiled=True)
    col_sketch = lax.psum_scatter(col_part, ("bx", "bz"), scatter_dimension=1, tiled=True)
    shrunk = jnp.einsum("pij,bj->pib", slab, core_cols, precision=highest)
    reduced = lax.psum_scatter(shrunk, "by", scatter_dimension=2, tiled=True)
    partial_value = jnp.einsum("pib,ai->pab", reduced, core_rows, precision=highest)
    partial_value = lax.psum_scatter(partial_value, "bx", scatter_dimension=1, tiled=True)
    core_sketch = jnp.einsum(
        "cp,pab->cab",
        core_planes,
        lax.all_gather(partial_value, "bz", axis=0, tiled=True),
        precision=highest,
    )
    return (plane_sketch, row_sketch, col_sketch, core_sketch)


def solution(mesh):
    in_specs = (
        P(("groups", "bz"), "bx", "by"),
        P("bz", None),
        P("bx", None),
        P("by", None),
        P("bz", None),
        P(None, "bx"),
        P(None, "by"),
    )
    out_specs = (
        P(("groups", "bz"), None),
        P(("groups", "bx"), ("by", "bz")),
        P(("groups", "by"), ("bx", "bz")),
        P(("groups", "bz"), "bx", "by"),
    )
    return jax.shard_map(
        on_device, mesh=mesh, in_specs=in_specs, out_specs=out_specs, check_vma=False
    )
```

profile of v0, /device:TPU:0, one launch (start us, length us, event | category | flops | bytes accessed | tf_op | source)
XLA Modules:
  0.0 129.5 jit_solution(7191022147818254434)
XLA Ops:
  7.2 0.0 copy-start
  7.2 0.0 reduce-scatter.9.cloned.1.call-start
  7.2 1.2 copy-done
  8.4 2.8 %convolution_bitcast_fusion.2 = f32[1,128,512]{2,1,0:T(8,128)} fusion(f32[512,512]{1,0:T(8,128)S(1)} %copy-done, f32[1,128,512]{2,1,0:T(8,128)} %param.7), kind=kOutput, calls=%fused_computation.4 | convolution fusion | flops 402653184 | bytes 1572864 | tf_op jit(solution)/shard_map/pij,bj->pib/dot_general | solution.py:17
  11.2 0.0 reduce-scatter.9.cloned.1.call-update
  11.2 0.0 reduce-scatter.11.cloned.1.call-start
  11.3 14.5 %reduce-scatter.9.cloned.1.call-done = f32[1,128,256]{2,1,0:T(8,128)} async-done(((f32[1,128,512]{2,1,0:T(8,128)}), f32[1,128,256]{2,1,0:T(8,128)}) %reduce-scatter.9.cloned.1.call-update) | async-done | bytes 131088 | tf_op jit(solution)/shard_map/reduce_scatter | solution.py:18
  25.8 2.4 %convolution_bitcast_fusion.1 = f32[1,512,256]{1,2,0:T(8,128)} fusion(f32[512,128]{1,0:T(8,128)} %param.12, f32[1,128,256]{2,1,0:T(8,128)} %reduce-scatter.9.cloned.1.call-done), kind=kOutput, calls=%fused_computation.1 | convolution fusion | flops 201326592 | bytes 917504 | tf_op jit(solution)/shard_map/pib,ai->pab/dot_general | solution.py:19
  28.2 0.0 reduce-scatter.11.cloned.1.call-update
  28.2 0.0 reduce-scatter.13.cloned.1.call-start
  28.3 1.6 %multiply_reduce_fusion = (f32[256]{0:T(256)S(1)}, f32[128,256]{1,0:T(8,128)S(1)}) fusion(f32[128,256]{1,0:T(8,128)} %param.9, f32[512,256]{1,0:T(8,128)} %param.10, f32[1,128,512]{2,1,0:T(8,128)} %param.7), kind=kOutput, calls=%fused_computation.11 | convolution fusion | flops 201391872 | bytes 1049600 | tf_op jit(solution)/shard_map/pij,jr->pir/dot_general | solution.py:9
  29.9 0.7 broadcast_multiply_fusion
  30.5 0.7 copy.24
  31.3 0.0 reduce-scatter.13.cloned.1.call-update
  31.3 0.0 reduce-scatter.7.cloned.1.call-start
  31.4 2.4 %fusion = f32[512,256]{0,1:T(8,128)} fusion(f32[128,256]{1,0:T(8,128)} %param.9, f32[1,128,512]{2,1,0:T(8,128)} %param.7, f32[256]{0:T(256)} %bitcast.40), kind=kOutput, calls=%fused_computation.3 | convolution fusion | flops 201457664 | bytes 918528 | tf_op jit(solution)/shard_map/pij,ir->pjr/dot_general | solution.py:12
  33.8 0.0 reduce-scatter.7.cloned.1.call-update
  33.8 21.1 %psum.7 = f32[1,256]{1,0:T(1,128)} all-reduce(f32[1,256]{1,0:T(1,128)S(1)} %bitcast.38), channel_id=1, replica_groups=mesh['groups'=2,'bx'=4,'by'=2,'bz'=2] {'bx','by'}, use_global_device_ids=true, to_apply=%region_0.0 | all-reduce | flops 256 | bytes 2048 | tf_op jit(solution)/shard_map/psum | solution.py:14
  54.9 0.0 reduce-scatter.11.cloned.1.call-done
  54.9 1.0 copy.14
  55.9 2.0 %all_gather.3 = f32[2,128,256]{2,1,0:T(8,128)S(1)} all-gather(f32[1,128,256]{2,1,0:T(8,128)S(1)} %copy.14), channel_id=1, replica_groups=mesh['groups'=2,'bx'=4,'by'=2,'bz'=2] {'bz'}, dimensions={0}, use_global_device_ids=true | all-gather | bytes 393216 | tf_op jit(solution)/shard_map/all_gather | solution.py:24
  57.9 0.0 copy-start.1
  57.9 30.9 %convolution_bitcast_fusion = f32[256,128,256]{0,2,1:T(8,128)} fusion(f32[2,128,256]{2,1,0:T(8,128)S(1)} %all_gather.3, f32[256,2]{0,1:T(2,128)} %param.11), kind=kOutput, calls=%fused_computation | convolution fusion | flops 201326592 | bytes 33818624 | tf_op jit(solution)/shard_map/cp,pab->cab/dot_general | solution.py:21
  88.8 34.1 %copy.17 = f32[256,128,256]{2,1,0:T(8,128)} copy(f32[256,128,256]{0,2,1:T(8,128)} %convolution_bitcast_fusion) | data formatting | bytes 67108864
  122.9 0.0 reduce-scatter.13.cloned.1.call-done
  122.9 0.0 reduce-scatter.7.cloned.1.call-done
  122.9 0.0 copy-done.1
Async XLA Ops:
  7.2 1.2 copy-start
  7.2 18.6 %reduce-scatter.9.cloned.1.call-start = ((), (), s32[]{:S(2)}) async-start(), calls=%async_computation.5 | async-start | bytes 393216 | tf_op jit(solution)/shard_map/reduce_scatter | solution.py:18
  11.2 43.6 %reduce-scatter.11.cloned.1.call-start = ((), (), s32[]{:S(2)}) async-start(), calls=%async_computation.6 | async-start | bytes 655360 | tf_op jit(solution)/shard_map/reduce_scatter | solution.py:20
  28.2 94.7 %reduce-scatter.13.cloned.1.call-start = ((), (), s32[]{:S(2)}) async-start(), calls=%async_computation.7 | async-start | bytes 163840
  31.3 91.6 %reduce-scatter.7.cloned.1.call-start = ((), (), s32[]{:S(2)}) async-start(), calls=%async_computation.4 | async-start | bytes 589824 | tf_op jit(solution)/shard_map/reduce_scatter | solution.py:16
  57.9 65.0 %copy-start.1 = (f32[512,512]{1,0:T(8,128)S(1)}, f32[512,512]{1,0:T(8,128)}, u32[]{:S(2)}) copy-start(f32[512,512]{1,0:T(8,128)} %param.13) | copy-start | bytes 3145732
Sparse Core Ops, SparseCore 0:
  11.4 14.3 reduce-scatter.8
  28.7 21.6 reduce-scatter.10
  53.5 17.8 reduce-scatter.12
  74.2 30.9 reduce-scatter.6
where the time goes:
time: 130 us; the launch traced here: 129 us
  matrix products  40.2 us (31%)
  local copies, waits for them, and re-layouts  37 us (28%)
  blocking collectives  23.1 us (18%)
  waiting for transfers between devices  14.5 us (11%)
  between operations  13.8 us (11%)
    unnamed x6, local copies, waits for them, and re-layouts  36 us
    dot_general x1, matrix products, on_device(): jnp.einsum('cp,pab->cab', core_planes, lax.all_gather(partial_value, 'bz'...  30.9 us
    psum x1, blocking collectives, on_device(): plane_sketch = lax.psum(plane_part, ('bx', 'by'))  21.1 us
    reduce_scatter x1, waiting for transfers between devices, on_device(): reduced = lax.psum_scatter(shrunk, 'by', scatter_dimension=2, tiled=True)  14.5 us
    dot_general x1, matrix products, on_device(): shrunk = jnp.einsum('pij,bj->pib', slab, core_cols, precision=highest)  2.83 us
  transfers between devices with their start and end apart: 4, of which 1 were waited for; matrix products, arithmetic and copies ran while one was open for 55% of the time, Pallas kernels for 0%

commit v1 on v0

--- a/solution.py
+++ b/solution.py
@@ -11,7 +11,7 @@
     row_part = jnp.einsum("pir,pr->ir", by_col, plane_test, precision=highest)
     by_row = jnp.einsum("pij,ir->pjr", slab, row_test, precision=highest)
     col_part = jnp.einsum("pjr,pr->jr", by_row, plane_test, precision=highest)
-    plane_sketch = lax.psum(plane_part, ("bx", "by"))
+    plane_sketch = lax.psum(lax.psum(plane_part, "by"), "bx")
     row_sketch = lax.psum_scatter(row_part, ("by", "bz"), scatter_dimension=1, tiled=True)
     col_sketch = lax.psum_scatter(col_part, ("bx", "bz"), scatter_dimension=1, tiled=True)
     shrunk = jnp.einsum("pij,bj->pib", slab, core_cols, precision=highest)

time: 130 us -> 127 us (0.977)
  blocking collectives: 23.1 us -> 19.5 us
    psum x1 -> x2, blocking collectives: 21.1 us -> 17.5 us  [on_device(): plane_sketch = lax.psum(lax.psum(plane_part, 'by'), 'bx')]
  transfers between devices with their start and end apart: 4 -> 4, of which waited for: 1 -> 1; matrix products, arithmetic and copies ran while one was open for 55% -> 57% of each run, Pallas kernels for 0% -> 0%
where the time goes in v1:
time: 127 us; the launch traced here: 126 us
  matrix products  40.2 us (32%)
  local copies, waits for them, and re-layouts  37.1 us (29%)
  blocking collectives  19.5 us (15%)
  waiting for transfers between devices  14.5 us (11%)
  between operations  13.8 us (11%)
    unnamed x6, local copies, waits for them, and re-layouts  36.1 us
    dot_general x1, matrix products, on_device(): jnp.einsum('cp,pab->cab', core_planes, lax.all_gather(partial_value, 'bz'...  30.9 us
    psum x2, blocking collectives, on_device(): plane_sketch = lax.psum(lax.psum(plane_part, 'by'), 'bx')  17.5 us
    reduce_scatter x1, waiting for transfers between devices, on_device(): reduced = lax.psum_scatter(shrunk, 'by', scatter_dimension=2, tiled=True)  14.5 us
    dot_general x1, matrix products, on_device(): shrunk = jnp.einsum('pij,bj->pib', slab, core_cols, precision=highest)  2.83 us
  transfers between devices with their start and end apart: 4, of which 1 were waited for; matrix products, arithmetic and copies ran while one was open for 57% of the time, Pallas kernels for 0%

profile of v1, /device:TPU:0, one launch (start us, length us, event | category | flops | bytes accessed | tf_op | source)
XLA Modules:
  0.0 126.0 jit_solution(11391477965267706261)
XLA Ops:
  7.2 0.0 copy-start
  7.2 0.0 reduce-scatter.9.cloned.1.call-start
  7.2 1.2 copy-done
  8.4 2.8 %convolution_bitcast_fusion.2 = f32[1,128,512]{2,1,0:T(8,128)} fusion(f32[512,512]{1,0:T(8,128)S(1)} %copy-done, f32[1,128,512]{2,1,0:T(8,128)} %param.7), kind=kOutput, calls=%fused_computation.4 | convolution fusion | flops 402653184 | bytes 1572864 | tf_op jit(solution)/shard_map/pij,bj->pib/dot_general | solution.py:17
  11.2 0.0 reduce-scatter.9.cloned.1.call-update
  11.2 0.0 reduce-scatter.11.cloned.1.call-start
  11.3 14.5 %reduce-scatter.9.cloned.1.call-done = f32[1,128,256]{2,1,0:T(8,128)} async-done(((f32[1,128,512]{2,1,0:T(8,128)}), f32[1,128,256]{2,1,0:T(8,128)}) %reduce-scatter.9.cloned.1.call-update) | async-done | bytes 131088 | tf_op jit(solution)/shard_map/reduce_scatter | solution.py:18
  25.8 2.4 %convolution_bitcast_fusion.1 = f32[1,512,256]{1,2,0:T(8,128)} fusion(f32[512,128]{1,0:T(8,128)} %param.12, f32[1,128,256]{2,1,0:T(8,128)} %reduce-scatter.9.cloned.1.call-done), kind=kOutput, calls=%fused_computation.1 | convolution fusion | flops 201326592 | bytes 917504 | tf_op jit(solution)/shard_map/pib,ai->pab/dot_general | solution.py:19
  28.2 0.0 reduce-scatter.11.cloned.1.call-update
  28.2 0.0 reduce-scatter.13.cloned.1.call-start
  28.3 1.6 %multiply_reduce_fusion = (f32[256]{0:T(256)S(1)}, f32[128,256]{1,0:T(8,128)S(1)}) fusion(f32[128,256]{1,0:T(8,128)} %param.9, f32[512,256]{1,0:T(8,128)} %param.10, f32[1,128,512]{2,1,0:T(8,128)} %param.7), kind=kOutput, calls=%fused_computation.11 | convolution fusion | flops 201391872 | bytes 1049600 | tf_op jit(solution)/shard_map/pij,jr->pir/dot_general | solution.py:9
  29.9 0.7 broadcast_multiply_fusion
  30.5 0.7 copy.24
  31.3 0.0 reduce-scatter.13.cloned.1.call-update
  31.3 0.0 reduce-scatter.7.cloned.1.call-start
  31.4 2.4 %fusion = f32[512,256]{0,1:T(8,128)} fusion(f32[128,256]{1,0:T(8,128)} %param.9, f32[1,128,512]{2,1,0:T(8,128)} %param.7, f32[256]{0:T(256)} %bitcast.40), kind=kOutput, calls=%fused_computation.3 | convolution fusion | flops 201457664 | bytes 918528 | tf_op jit(solution)/shard_map/pij,ir->pjr/dot_general | solution.py:12
  33.8 0.0 reduce-scatter.7.cloned.1.call-update
  33.8 4.9 %psum.14 = f32[1,256]{1,0:T(1,128)S(1)} all-reduce(f32[1,256]{1,0:T(1,128)S(1)} %bitcast.38), channel_id=1, replica_groups=mesh['groups'=2,'bx'=4,'by'=2,'bz'=2] {'by'}, use_global_device_ids=true, to_apply=%region_0.0 | all-reduce | flops 256 | bytes 2048 | tf_op jit(solution)/shard_map/psum | solution.py:14
  38.7 12.6 %psum.15 = f32[1,256]{1,0:T(1,128)} all-reduce(f32[1,256]{1,0:T(1,128)S(1)} %psum.14), channel_id=1, replica_groups=mesh['groups'=2,'bx'=4,'by'=2,'bz'=2] {'bx'}, use_global_device_ids=true, to_apply=%region_1.0 | all-reduce | flops 256 | bytes 2048 | tf_op jit(solution)/shard_map/psum | solution.py:14
  51.3 0.0 reduce-scatter.11.cloned.1.call-done
  51.3 1.0 copy.14
  52.3 2.0 %all_gather.3 = f32[2,128,256]{2,1,0:T(8,128)S(1)} all-gather(f32[1,128,256]{2,1,0:T(8,128)S(1)} %copy.14), channel_id=1, replica_groups=mesh['groups'=2,'bx'=4,'by'=2,'bz'=2] {'bz'}, dimensions={0}, use_global_device_ids=true | all-gather | bytes 393216 | tf_op jit(solution)/shard_map/all_gather | solution.py:24
  54.3 0.0 copy-start.1
  54.3 30.9 %convolution_bitcast_fusion = f32[256,128,256]{0,2,1:T(8,128)} fusion(f32[2,128,256]{2,1,0:T(8,128)S(1)} %all_gather.3, f32[256,2]{0,1:T(2,128)} %param.11), kind=kOutput, calls=%fused_computation | convolution fusion | flops 201326592 | bytes 33818624 | tf_op jit(solution)/shard_map/cp,pab->cab/dot_general | solution.py:21
  85.3 34.2 %copy.17 = f32[256,128,256]{2,1,0:T(8,128)} copy(f32[256,128,256]{0,2,1:T(8,128)} %convolution_bitcast_fusion) | data formatting | bytes 67108864
  119.4 0.0 reduce-scatter.13.cloned.1.call-done
  119.4 0.0 reduce-scatter.7.cloned.1.call-done
  119.4 0.0 copy-done.1
Async XLA Ops:
  7.2 1.2 copy-start
  7.2 18.6 %reduce-scatter.9.cloned.1.call-start = ((), (), s32[]{:S(2)}) async-start(), calls=%async_computation.5 | async-start | bytes 393216 | tf_op jit(solution)/shard_map/reduce_scatter | solution.py:18
  11.2 40.1 %reduce-scatter.11.cloned.1.call-start = ((), (), s32[]{:S(2)}) async-start(), calls=%async_computation.6 | async-start | bytes 655360 | tf_op jit(solution)/shard_map/reduce_scatter | solution.py:20
  28.2 91.2 %reduce-scatter.13.cloned.1.call-start = ((), (), s32[]{:S(2)}) async-start(), calls=%async_computation.7 | async-start | bytes 163840
  31.3 88.1 %reduce-scatter.7.cloned.1.call-start = ((), (), s32[]{:S(2)}) async-start(), calls=%async_computation.4 | async-start | bytes 589824 | tf_op jit(solution)/shard_map/reduce_scatter | solution.py:16
  54.3 65.1 %copy-start.1 = (f32[512,512]{1,0:T(8,128)S(1)}, f32[512,512]{1,0:T(8,128)}, u32[]{:S(2)}) copy-start(f32[512,512]{1,0:T(8,128)} %param.13) | copy-start | bytes 3145732
Sparse Core Ops, SparseCore 0:
  11.4 14.3 reduce-scatter.8
  28.7 21.7 reduce-scatter.10
  53.6 17.8 reduce-scatter.12
  74.2 30.9 reduce-scatter.6
